TPU v7x, 32 devices: a whole 2x2x4 slice. The times are simulated.
32 devices in a mesh: row: 8 (over z, core), col: 4 (over y, x).
Axes of the slice: x: 2, y: 2, z: 4, core: 2. Of those that a mesh axis runs over, the one named last changes fastest.
Arguments:
- grad: bfloat16 [2, 6144, 24576], P(None, 'row', 'col'), may hold values from -45 to 45, as said below
- memory: float32 [2, 6144, 24576], P(None, 'row', 'col'), may hold values from -6 to 6
- p_prev: float32 [2, 6144, 32], P(None, ('row', 'col')), may hold values from -6 to 6
- q_prev: float32 [2, 24576, 32], P(None, ('col', 'row')), may hold values from -1 to 1
Outputs:
- p_new: float32 [2, 6144, 32], P(None, ('row', 'col'))
- q_new: float32 [2, 24576, 32], P(None, ('col', 'row'))
- error: float32 [2, 6144, 24576], P(None, 'row', 'col')
Inputs may be any that keep to these rules, and one draw needn't show every extreme that they name: `grad`: real-valued gradient entries.
All inputs are finite; a program needn't handle non-finite values.
Results may differ from a plain program's by a relative error of at most 0.0003.
Values sent between devices are 32-bit elements; how exact they have to be, the bound alone decides.
A program may use at most 192 MiB of HBM per device.

v0:
```python
import jax
import jax.numpy as jnp
from jax import lax
from jax.sharding import PartitionSpec as P


def shards(grad, memory, p_prev, q_prev):
    highest = lax.Precision.HIGHEST
    left_rows = lax.all_gather(p_prev, "col", axis=1, tiled=True)
    right_rows = lax.all_gather(q_prev, "row", axis=1, tiled=True)
    approx = jnp.einsum("lrk,lck->lrc", left_rows, right_rows, precision=highest)
    merged = grad.astype(jnp.float32) + memory - approx
    partial_value = jnp.einsum("lrc,lck->lrk", merged, right_rows, precision=highest)
    left = lax.psum(partial_value, "col")
    gram_part = jnp.einsum("lrk,lrj->lkj", left, left, precision=highest)
    gram = lax.psum(gram_part, "row")
    factor = jnp.linalg.cholesky(gram)
    p_hat = lax.linalg.triangular_solve(factor, left, left_side=False, lower=True, transpose_a=True)
    right_part = jnp.einsum("lrc,lrk->lck", merged, p_hat, precision=highest)
    share_rows = right_part.shape[1] // lax.axis_size("row")
    right_full = lax.psum(right_part, "row")
    q_new = lax.dynamic_slice_in_dim(right_full, lax.axis_index("row") * share_rows, share_rows, 1)
    error = merged - jnp.einsum("lrk,lck->lrc", p_hat, right_full, precision=highest)
    left_share = p_hat.shape[1] // lax.axis_size("col")
    p_new = lax.dynamic_slice_in_dim(p_hat, lax.axis_index("col") * left_share, left_share, 1)
    return (p_new, q_new, error)


def solution(mesh):
    placed = (
        P(None, "row", "col"),
        P(None, "row", "col"),
        P(None, ("row", "col"), None),
        P(None, ("col", "row"), None),
    )
    return jax.shard_map(
        shards,
        mesh=mesh,
        in_specs=placed,
        out_specs=(
            P(None, ("row", "col"), None),
            P(None, ("col", "row"), None),
            P(None, "row", "col"),
        ),
        check_vma=False,
    )
```

profile of v0, /device:TPU:0, one launch (start us, length us, event | category | flops | bytes accessed | tf_op | source)
XLA Modules:
  0.0 335.4 jit_solution(1339748341165155115)
XLA Ops:
  7.2 0.0 all-gather.2.cloned.1.call-start
  7.2 0.7 all-gather.2.cloned.1.call-update
  7.9 0.0 all-reduce.3.cloned.1.call-start
  7.9 1.0 copy.15
  8.9 12.7 %all_gather.6 = f32[2,768,32]{2,0,1:T(2,128)S(1)} all-gather(f32[2,192,32]{2,0,1:T(2,128)S(1)} %copy.15), channel_id=1, replica_groups=mesh['row'=8,'col'=4] {'col'}, dimensions={1}, use_global_device_ids=true | all-gather | bytes 245760 | tf_op jit(solution)/shard_map/all_gather | solution.py:9
  21.6 16.0 %all-gather.2.cloned.1.call-done = f32[2,6144,32]{1,2,0:T(8,128)} async-done(((f32[2,768,32]{1,2,0:T(8,128)}), f32[2,6144,32]{1,2,0:T(8,128)}) %all-gather.2.cloned.1.call-update) | async-done | bytes 1572880 | tf_op jit(solution)/shard_map/all_gather | solution.py:10
  37.6 0.0 copy-start
  37.6 44.0 %add_subtract_fusion = f32[2,768,6144]{2,1,0:T(8,128)} fusion(f32[2,768,6144]{2,1,0:T(8,128)} %param.5, bf16[2,768,6144]{2,1,0:T(8,128)(2,1)} %param.4, f32[2,6144,32]{1,2,0:T(8,128)} %all-gather.2.cloned.1.call-done, f32[2,768,32]{2,0,1:T(2,128)S(1)} %all_gather.6), kind=kOutput, calls=%fused_computation | convolution fusion | flops 3652190208 | bytes 96141312 | tf_op jit(solution)/shard_map/lrk,lck->lrc/dot_general | solution.py:11
  81.6 0.0 copy-done
  81.6 39.0 %fusion.4 = f32[2,768,32]{1,2,0:T(8,128)} fusion(f32[2,768,6144]{2,1,0:T(8,128)} %add_subtract_fusion, f32[2,6144,32]{1,2,0:T(8,128)S(1)} %copy-done), kind=kOutput, calls=%fused_computation.14 | convolution fusion | flops 3623878656 | bytes 39518208 | tf_op jit(solution)/shard_map/lrc,lck->lrk/dot_general | solution.py:13
  120.5 0.0 all-reduce.3.cloned.1.call-update
  120.6 0.0 all-reduce.5.cloned.1.call-start
  120.6 41.8 %all-reduce.3.cloned.1.call-done = f32[2,768,32]{1,2,0:T(8,128)} async-done(((f32[2,768,32]{1,2,0:T(8,128)}), f32[2,768,32]{1,2,0:T(8,128)}) %all-reduce.3.cloned.1.call-update) | async-done | bytes 196624 | tf_op jit(solution)/shard_map/psum | solution.py:14
  162.4 1.3 fusion.5
  163.8 28.1 %psum.22 = f32[2,32,32]{1,2,0:T(8,128)S(1)} all-reduce(f32[2,32,32]{1,2,0:T(8,128)S(1)} %fusion.5), channel_id=1, replica_groups=mesh['row'=8,'col'=4] {'row'}, use_global_device_ids=true, to_apply=%region_1.0 | all-reduce | flops 2048 | bytes 16384 | tf_op jit(solution)/shard_map/psum | solution.py:16
  191.9 0.1 copy.18
  192.0 5.9 %custom-call.7 = f32[2,32,32]{2,1,0:T(8,128)S(1)} custom-call(f32[2,32,32]{2,1,0:T(8,128)S(1)} %fusion.3), custom_call_target="Cholesky" | custom-call | tf_op jit(solution)/shard_map/jit(cholesky)/cholesky | solution.py:17
  197.9 0.1 compare_reduce_fusion
  198.0 0.1 select_bitcast_fusion
  198.1 4.9 %custom-call.8 = f32[2,1,32,32]{2,3,1,0:T(8,128)S(1)} custom-call(f32[2,1,32,32]{3,2,1,0:T(8,128)S(1)} %select_bitcast_fusion), custom_call_target="InvertDiagBlocksLowerTriangular" | custom-call | tf_op jit(solution)/shard_map/triangular_solve | solution.py:18
  203.0 1.3 fusion.1
  204.3 26.9 %fusion.6 = f32[2,6144,32]{1,2,0:T(8,128)} fusion(f32[2,768,6144]{2,1,0:T(8,128)} %add_subtract_fusion, f32[2,768,32]{1,2,0:T(8,128)S(1)} %fusion.1), kind=kOutput, calls=%fused_computation.16 | convolution fusion | flops 3623878656 | bytes 39518208 | tf_op jit(solution)/shard_map/lrc,lrk->lck/dot_general | solution.py:19
  231.2 0.0 all-reduce.5.cloned.1.call-update
  231.2 0.7 constant_dynamic-slice_fusion.1
  231.9 58.6 %all-reduce.5.cloned.1.call-done = f32[2,6144,32]{1,2,0:T(8,128)} async-done(((f32[2,6144,32]{1,2,0:T(8,128)}), f32[2,6144,32]{1,2,0:T(8,128)}) %all-reduce.5.cloned.1.call-update) | async-done | bytes 1572880 | tf_op jit(solution)/shard_map/psum | solution.py:21
  290.5 36.7 %convolution_subtract_fusion = f32[2,768,6144]{2,1,0:T(8,128)} fusion(f32[2,768,6144]{2,1,0:T(8,128)} %add_subtract_fusion, f32[2,768,32]{1,2,0:T(8,128)S(1)} %fusion.1, f32[2,6144,32]{1,2,0:T(8,128)} %all-reduce.5.cloned.1.call-done), kind=kOutput, calls=%fused_computation.1 | convolution fusion | flops 3633315840 | bytes 77266944 | tf_op jit(solution)/shard_map/lrk,lck->lrc/dot_general | solution.py:23
  327.2 1.6 constant_dynamic-slice_fusion
  (4 shorter events, 0.1 us)
Async XLA Ops:
  7.2 30.4 %all-gather.2.cloned.1.call-start = ((), (), s32[]{:S(2)}) async-start(), calls=%async_computation | async-start | bytes 1769472 | tf_op jit(solution)/shard_map/all_gather | solution.py:10
  7.9 154.5 %all-reduce.3.cloned.1.call-start = ((), (), s32[]{:S(2)}) async-start(), calls=%async_computation.1 | async-start | bytes 393216 | tf_op jit(solution)/shard_map/psum | solution.py:14
  37.6 44.0 %copy-start = (f32[2,6144,32]{1,2,0:T(8,128)S(1)}, f32[2,6144,32]{1,2,0:T(8,128)}, u32[]{:S(2)}) copy-start(f32[2,6144,32]{1,2,0:T(8,128)} %all-gather.2.cloned.1.call-done) | copy-start | bytes 4718596
  120.6 169.9 %all-reduce.5.cloned.1.call-start = ((), (), s32[]{:S(2)}) async-start(), calls=%async_computation.2 | async-start | bytes 3145728 | tf_op jit(solution)/shard_map/psum | solution.py:21
Sparse Core Ops, SparseCore 0:
  9.6 27.9 all-gather.1
  120.7 41.7 all-reduce.2
  231.3 59.1 all-reduce.4
where the time goes:
time: 336 us; the launch traced here: 335 us
  matrix products  149 us (44%)
  waiting for transfers between devices  117 us (35%)
  blocking collectives  40.8 us (12%)
  between operations  13.8 us (4%)
  other arithmetic  11 us (3%)
  local copies, waits for them, and re-layouts  3.39 us (1%)
    psum x1, waiting for transfers between devices, shards(): right_full = lax.psum(right_part, 'row')  58.6 us
    dot_general x1, matrix products, shards(): jnp.einsum('lrk,lck->lrc', left_rows, right_rows, precision=highest)  44 us
    psum x1, waiting for transfers between devices, shards(): left = lax.psum(partial_value, 'col')  41.8 us
    dot_general x1, matrix products, shards(): jnp.einsum('lrc,lck->lrk', merged, right_rows, precision=highest)  39 us
    dot_general x1, matrix products, shards(): jnp.einsum('lrk,lck->lrc', p_hat, right_full, precision=highest)  36.7 us
    psum x1, blocking collectives, shards(): gram = lax.psum(gram_part, 'row')  28.1 us
    dot_general x1, matrix products, shards(): right_part = jnp.einsum('lrc,lrk->lck', merged, p_hat, precision=highest)  26.9 us
    all_gather x1, waiting for transfers between devices, shards(): right_rows = lax.all_gather(q_prev, 'row', axis=1, tiled=True)  16 us
  transfers between devices with their start and end apart: 3, of which 3 were waited for; matrix products, arithmetic and copies ran while one was open for 1% of the time, Pallas kernels for 0%

commit v1 on v0

--- a/solution.py
+++ b/solution.py
@@ -13,7 +13,8 @@
     partial_value = jnp.einsum("lrc,lck->lrk", merged, right_rows, precision=highest)
     left = lax.psum(partial_value, "col")
     gram_part = jnp.einsum("lrk,lrj->lkj", left, left, precision=highest)
-    gram = lax.psum(gram_part, "row")
+    upper = lax.all_gather(gram_part, axis_name="row")
+    gram = jnp.sum(upper, axis=0)
     factor = jnp.linalg.cholesky(gram)
     p_hat = lax.linalg.triangular_solve(factor, left, left_side=False, lower=True, transpose_a=True)
     right_part = jnp.einsum("lrc,lrk->lck", merged, p_hat, precision=highest)

time: 336 us -> 325 us (0.967)
  blocking collectives: 40.8 us -> 26.9 us
    psum x1 -> x0, blocking collectives: 28.1 us -> none  [shards(): gram = lax.psum(gram_part, 'row')]
    all_gather x0 -> x1, blocking collectives: none -> 14.3 us  [shards(): upper = lax.all_gather(gram_part, axis_name='row')]
where the time goes in v1:
time: 325 us; the launch traced here: 324 us
  matrix products  149 us (46%)
  waiting for transfers between devices  120 us (37%)
  blocking collectives  26.9 us (8%)
  between operations  13.8 us (4%)
  other arithmetic  11.3 us (3%)
  local copies, waits for them, and re-layouts  3.39 us (1%)
    psum x1, waiting for transfers between devices, shards(): right_full = lax.psum(right_part, 'row')  61.3 us
    dot_general x1, matrix products, shards(): jnp.einsum('lrk,lck->lrc', left_rows, right_rows, precision=highest)  44 us
    psum x1, waiting for transfers between devices, shards(): left = lax.psum(partial_value, 'col')  41.8 us
    dot_general x1, matrix products, shards(): jnp.einsum('lrc,lck->lrk', merged, right_rows, precision=highest)  39 us
    dot_general x1, matrix products, shards(): jnp.einsum('lrk,lck->lrc', p_hat, right_full, precision=highest)  36.7 us
    dot_general x1, matrix products, shards(): right_part = jnp.einsum('lrc,lrk->lck', merged, p_hat, precision=highest)  26.9 us
    all_gather x1, waiting for transfers between devices, shards(): right_rows = lax.all_gather(q_prev, 'row', axis=1, tiled=True)  16 us
    all_gather x1, blocking collectives, shards(): upper = lax.all_gather(gram_part, axis_name='row')  14.3 us
  transfers between devices with their start and end apart: 3, of which 3 were waited for; matrix products, arithmetic and copies ran while one was open for 1% of the time, Pallas kernels for 0%

profile of v1, /device:TPU:0, one launch (start us, length us, event | category | flops | bytes accessed | tf_op | source)
XLA Modules:
  0.0 324.5 jit_solution(15090341324582823974)
XLA Ops:
  7.2 0.0 all-gather.3.cloned.1.call-start
  7.2 0.7 all-gather.3.cloned.1.call-update
  7.9 0.0 all-reduce.3.cloned.1.call-start
  7.9 1.0 copy.13
  8.9 12.7 %all_gather.12 = f32[2,768,32]{2,0,1:T(2,128)S(1)} all-gather(f32[2,192,32]{2,0,1:T(2,128)S(1)} %copy.13), channel_id=1, replica_groups=mesh['row'=8,'col'=4] {'col'}, dimensions={1}, use_global_device_ids=true | all-gather | bytes 245760 | tf_op jit(solution)/shard_map/all_gather | solution.py:9
  21.6 16.0 %all-gather.3.cloned.1.call-done = f32[2,6144,32]{1,2,0:T(8,128)} async-done(((f32[2,768,32]{1,2,0:T(8,128)}), f32[2,6144,32]{1,2,0:T(8,128)}) %all-gather.3.cloned.1.call-update) | async-done | bytes 1572880 | tf_op jit(solution)/shard_map/all_gather | solution.py:10
  37.6 0.0 copy-start
  37.6 44.0 %add_subtract_fusion = f32[2,768,6144]{2,1,0:T(8,128)} fusion(f32[2,768,6144]{2,1,0:T(8,128)} %param.5, bf16[2,768,6144]{2,1,0:T(8,128)(2,1)} %param.4, f32[2,6144,32]{1,2,0:T(8,128)} %all-gather.3.cloned.1.call-done, f32[2,768,32]{2,0,1:T(2,128)S(1)} %all_gather.12), kind=kOutput, calls=%fused_computation | convolution fusion | flops 3652190208 | bytes 96141312 | tf_op jit(solution)/shard_map/lrk,lck->lrc/dot_general | solution.py:11
  81.6 0.0 copy-done
  81.6 39.0 %fusion.4 = f32[2,768,32]{1,2,0:T(8,128)} fusion(f32[2,768,6144]{2,1,0:T(8,128)} %add_subtract_fusion, f32[2,6144,32]{1,2,0:T(8,128)S(1)} %copy-done), kind=kOutput, calls=%fused_computation.14 | convolution fusion | flops 3623878656 | bytes 39518208 | tf_op jit(solution)/shard_map/lrc,lck->lrk/dot_general | solution.py:13
  120.5 0.0 all-reduce.3.cloned.1.call-update
  120.6 0.0 all-reduce.5.cloned.1.call-start
  120.6 41.8 %all-reduce.3.cloned.1.call-done = f32[2,768,32]{1,2,0:T(8,128)} async-done(((f32[2,768,32]{1,2,0:T(8,128)}), f32[2,768,32]{1,2,0:T(8,128)}) %all-reduce.3.cloned.1.call-update) | async-done | bytes 196624 | tf_op jit(solution)/shard_map/psum | solution.py:14
  162.4 1.3 fusion.5
  163.8 14.3 %all-gather = f32[16,32,32]{2,1,0:T(8,128)S(1)} all-gather(f32[2,32,32]{2,1,0:T(8,128)S(1)} %fusion.5), channel_id=2, replica_groups=mesh['row'=8,'col'=4] {'row'}, dimensions={0}, use_global_device_ids=true | all-gather | bytes 73728 | tf_op jit(solution)/shard_map/all_gather | solution.py:16
  178.0 0.1 copy.15
  178.1 6.1 %custom-call.7 = f32[2,32,32]{2,1,0:T(8,128)S(1)} custom-call(f32[2,32,32]{2,1,0:T(8,128)S(1)} %fusion.3), custom_call_target="Cholesky" | custom-call | tf_op jit(solution)/shard_map/jit(cholesky)/cholesky | solution.py:18
  184.3 0.1 compare_reduce_fusion
  184.4 0.1 select_bitcast_fusion
  184.5 4.9 %custom-call.8 = f32[2,1,32,32]{2,3,1,0:T(8,128)S(1)} custom-call(f32[2,1,32,32]{3,2,1,0:T(8,128)S(1)} %select_bitcast_fusion), custom_call_target="InvertDiagBlocksLowerTriangular" | custom-call | tf_op jit(solution)/shard_map/triangular_solve | solution.py:19
  189.4 1.3 fusion.1
  190.7 26.9 %fusion.6 = f32[2,6144,32]{1,2,0:T(8,128)} fusion(f32[2,768,6144]{2,1,0:T(8,128)} %add_subtract_fusion, f32[2,768,32]{1,2,0:T(8,128)S(1)} %fusion.1), kind=kOutput, calls=%fused_computation.16 | convolution fusion | flops 3623878656 | bytes 39518208 | tf_op jit(solution)/shard_map/lrc,lrk->lck/dot_general | solution.py:20
  217.6 0.0 all-reduce.5.cloned.1.call-update
  217.6 0.7 constant_dynamic-slice_fusion.1
  218.3 61.3 %all-reduce.5.cloned.1.call-done = f32[2,6144,32]{1,2,0:T(8,128)} async-done(((f32[2,6144,32]{1,2,0:T(8,128)}), f32[2,6144,32]{1,2,0:T(8,128)}) %all-reduce.5.cloned.1.call-update) | async-done | bytes 1572880 | tf_op jit(solution)/shard_map/psum | solution.py:22
  279.6 36.7 %convolution_subtract_fusion = f32[2,768,6144]{2,1,0:T(8,128)} fusion(f32[2,768,6144]{2,1,0:T(8,128)} %add_subtract_fusion, f32[2,768,32]{1,2,0:T(8,128)S(1)} %fusion.1, f32[2,6144,32]{1,2,0:T(8,128)} %all-reduce.5.cloned.1.call-done), kind=kOutput, calls=%fused_computation.1 | convolution fusion | flops 3633315840 | bytes 77266944 | tf_op jit(solution)/shard_map/lrk,lck->lrc/dot_general | solution.py:24
  316.3 1.6 constant_dynamic-slice_fusion
  (5 shorter events, 0.1 us)
Async XLA Ops:
  7.2 30.4 %all-gather.3.cloned.1.call-start = ((), (), s32[]{:S(2)}) async-start(), calls=%async_computation | async-start | bytes 1769472 | tf_op jit(solution)/shard_map/all_gather | solution.py:10
  7.9 154.5 %all-reduce.3.cloned.1.call-start = ((), (), s32[]{:S(2)}) async-start(), calls=%async_computation.1 | async-start | bytes 393216 | tf_op jit(solution)/shard_map/psum | solution.py:14
  37.6 44.0 %copy-start = (f32[2,6144,32]{1,2,0:T(8,128)S(1)}, f32[2,6144,32]{1,2,0:T(8,128)}, u32[]{:S(2)}) copy-start(f32[2,6144,32]{1,2,0:T(8,128)} %all-gather.3.cloned.1.call-done) | copy-start | bytes 4718596
  120.6 159.0 %all-reduce.5.cloned.1.call-start = ((), (), s32[]{:S(2)}) async-start(), calls=%async_computation.2 | async-start | bytes 3145728 | tf_op jit(solution)/shard_map/psum | solution.py:22
Sparse Core Ops, SparseCore 0:
  9.6 27.9 all-gather.2
  120.7 41.7 all-reduce.2
  217.7 61.8 all-reduce.4
